TPU v7x, 512 devices: a whole 4x8x8 slice. The times are simulated.
512 devices in a mesh: shot: 8 (over z_hi, x), recv: 8 (over y), surf: 8 (over z_lo, core).
Axes of the slice: x: 4, y: 8, z: 8 (z_hi: 2, z_lo: 4; z = z_hi * 4 + z_lo), core: 2. Of those that a mesh axis runs over, the one named last changes fastest.
Arguments:
- shot_data: bfloat16 [8, 2, 6144, 2048], P(None, None, ('surf', 'recv'), 'shot'), may hold values from -6 to 6
- recv_data: bfloat16 [8, 2, 6144, 2048], P(None, None, ('surf', 'shot'), 'recv'), may hold values from -0.078125 to 0.078125
- shot_offset: int32 [2048], P('shot'), may hold values from -256 to 255
- recv_offset: int32 [2048], P('recv'), may hold values from -256 to 255
- shot_taper_index: int32 [2048], P('shot'), may hold values from 0 to 3
- receiver_taper_index: int32 [2048], P('recv'), may hold values from 0 to 3
Outputs:
- predicted: float32 [8, 2, 2048, 2048], P('surf', None, 'shot', 'recv')
All inputs are finite; a program needn't handle non-finite values.
Results may differ from a plain program's by a relative error of at most 0.0003.
Values may be sent and summed in bfloat16 or wider, within the bound.
A program may use at most 64 MiB of HBM per device.

v0:
```python
import jax
import jax.numpy as jnp
from jax import lax
from jax.sharding import PartitionSpec as P

R = 2048


def panel_product(left_operand, right_operand):
    real_real = jnp.einsum(
        "xaq,xad->xqd", left_operand[:, 0], right_operand[:, 0], preferred_element_type=jnp.float32
    )
    imag_imag = jnp.einsum(
        "xaq,xad->xqd", left_operand[:, 1], right_operand[:, 1], preferred_element_type=jnp.float32
    )
    real_imag = jnp.einsum(
        "xaq,xad->xqd", left_operand[:, 0], right_operand[:, 1], preferred_element_type=jnp.float32
    )
    imag_real = jnp.einsum(
        "xaq,xad->xqd", left_operand[:, 1], right_operand[:, 0], preferred_element_type=jnp.float32
    )
    return jnp.stack([real_real - imag_imag, real_imag + imag_real], axis=1)


def make_folder(right_full, piece):
    return panel_product(piece, right_full)


def on_device(
    shot_data, recv_data, shot_offset, recv_offset, shot_taper_index, receiver_taper_index
):
    right_full = lax.all_gather(recv_data, "shot", axis=2, tiled=True)
    partial_sum = make_folder(right_full, lax.all_gather(shot_data, "recv", axis=2, tiled=True))
    multiples = lax.psum_scatter(partial_sum, "surf", scatter_dimension=0, tiled=True)
    shot_row_block = shot_offset.shape[0]
    recv_cols = recv_offset.shape[0]
    shot_pos = (
        lax.axis_index("shot") * shot_row_block
        + jnp.arange(shot_row_block, dtype=jnp.int32)
        + shot_offset
    )
    recv_pos = (
        lax.axis_index("recv") * recv_cols + jnp.arange(recv_cols, dtype=jnp.int32) + recv_offset
    )
    distance = jnp.abs(recv_pos[None, :] - shot_pos[:, None])
    half_width = R // 8 * (2 + shot_taper_index[:, None] + receiver_taper_index[None, :])
    ratio = jnp.minimum(distance, half_width).astype(jnp.float32) / half_width.astype(jnp.float32)
    taper = 0.5 * (1.0 + jnp.cos(jnp.pi * ratio))
    return multiples * taper[None, None, :, :]


def solution(mesh):
    placed = (
        P(None, None, ("surf", "recv"), "shot"),
        P(None, None, ("surf", "shot"), "recv"),
        P("shot"),
        P("recv"),
        P("shot"),
        P("recv"),
    )
    return jax.shard_map(
        on_device,
        mesh=mesh,
        in_specs=placed,
        out_specs=P("surf", None, "shot", "recv"),
        check_vma=False,
    )
```

profile of v0, /device:TPU:2, one launch (start us, length us, event | category | flops | bytes accessed | tf_op | source)
XLA Modules:
  0.0 370.5 jit_solution(3620094551108705786)
XLA Ops:
  6.5 0.0 all-gather.3.cloned.1.call-start
  6.5 2.5 copy.10
  9.1 0.0 all-gather.3.cloned.1.call-update
  9.1 0.0 all-gather.5.cloned.1.call-start
  9.1 2.1 copy.12
  11.2 0.0 all-gather.5.cloned.1.call-update
  11.2 0.0 all-reduce.3.cloned.1.call-start
  11.3 79.5 %all-gather.3.cloned.1.call-done = bf16[8,2,768,256]{3,0,1,2:T(8,128)(2,1)} async-done(((bf16[8,2,96,256]{3,0,1,2:T(8,128)(2,1)}), bf16[8,2,768,256]{3,0,1,2:T(8,128)(2,1)}) %all-gather.3.cloned.1.call-update) | async-done | bytes 6291472 | tf_op jit(solution)/shard_map/all_gather | solution.py:33
  90.8 5.9 %fusion.13 = (bf16[8,1,768,256]{3,0,1,2:T(8,128)(2,1)}, bf16[8,1,768,256]{3,0,1,2:T(8,128)(2,1)}) fusion(bf16[8,2,768,256]{3,0,1,2:T(8,128)(2,1)} %all-gather.3.cloned.1.call-done), kind=kLoop, calls=%fused_computation.19 | loop fusion | bytes 12582912 | tf_op jit(solution)/shard_map/slice | solution.py:11
  96.7 3.8 %copy.17 = bf16[8,1,768,256]{2,3,0,1:T(8,128)(2,1)S(1)} copy(bf16[8,1,768,256]{3,0,1,2:T(8,128)(2,1)} %get-tuple-element.5) | data formatting | bytes 6291456
  100.5 5.0 %copy.18 = bf16[8,1,768,256]{2,3,0,1:T(8,128)(2,1)} copy(bf16[8,1,768,256]{3,0,1,2:T(8,128)(2,1)} %get-tuple-element.6) | data formatting | bytes 6291456
  105.5 131.8 %all-gather.5.cloned.1.call-done = bf16[8,2,768,256]{3,2,0,1:T(8,128)(2,1)} async-done(((bf16[8,2,96,256]{3,2,0,1:T(8,128)(2,1)}), bf16[8,2,768,256]{3,2,0,1:T(8,128)(2,1)}) %all-gather.5.cloned.1.call-update) | async-done | bytes 6291472 | tf_op jit(solution)/shard_map/all_gather | solution.py:32
  237.3 0.0 copy-start
  237.3 4.0 %fusion = f32[8,256,256]{2,1,0:T(8,128)S(1)} fusion(bf16[8,1,768,256]{2,3,0,1:T(8,128)(2,1)} %copy.18, bf16[8,2,768,256]{3,2,0,1:T(8,128)(2,1)} %all-gather.5.cloned.1.call-done), kind=kOutput, calls=%fused_computation.3 | convolution fusion | flops 805306368 | bytes 8388608 | tf_op jit(solution)/shard_map/xaq,xad->xqd/dot_general | solution.py:19
  241.3 0.7 copy-done
  242.0 2.9 fusion.2
  244.8 1.0 subtract_bitcast_fusion
  245.8 1.0 add_bitcast_fusion
  246.8 2.3 pad_maximum_fusion
  249.2 0.0 copy-start.4
  249.2 0.0 copy-start.2
  249.2 0.0 copy-start.3
  249.2 0.0 copy-start.1
  249.2 0.0 all-reduce.3.cloned.1.call-update
  249.2 1.3 dynamic-slice
  250.6 0.0 copy-done.4
  250.6 0.0 copy-done.2
  250.6 0.0 copy-done.3
  250.6 0.0 copy-done.1
  250.6 1.1 add_multiply_fusion
  251.7 109.8 %all-reduce.3.cloned.1.call-done = f32[8,2,256,256]{3,2,0,1:T(8,128)} async-done(((f32[8,2,256,256]{3,2,0,1:T(8,128)}), f32[8,2,256,256]{3,2,0,1:T(8,128)}) %all-reduce.3.cloned.1.call-update) | async-done | bytes 4194320
  361.5 2.5 fusion.12
  (2 shorter events, 0.0 us)
Async XLA Ops:
  6.5 84.3 %all-gather.3.cloned.1.call-start = ((), (), s32[]{:S(2)}) async-start(), calls=%async_computation | async-start | bytes 7077888 | tf_op jit(solution)/shard_map/all_gather | solution.py:33
  9.1 228.3 %all-gather.5.cloned.1.call-start = ((), (), s32[]{:S(2)}) async-start(), calls=%async_computation.1 | async-start | bytes 7077888 | tf_op jit(solution)/shard_map/all_gather | solution.py:32
  11.2 350.3 %all-reduce.3.cloned.1.call-start = ((), (), s32[]{:S(2)}) async-start(), calls=%async_computation.2 | async-start | bytes 8388608
  237.3 4.6 %copy-start = (bf16[8,2,768,256]{3,2,0,1:T(8,128)(2,1)S(1)}, bf16[8,2,768,256]{3,2,0,1:T(8,128)(2,1)}, u32[]{:S(2)}) copy-start(bf16[8,2,768,256]{3,2,0,1:T(8,128)(2,1)} %all-gather.5.cloned.1.call-done) | copy-start | bytes 18874372
  249.2 1.4 copy-start.4
  249.2 1.4 copy-start.2
  249.2 1.4 copy-start.3
  249.2 1.4 copy-start.1
Sparse Core Ops, SparseCore 0:
  9.4 81.3 all-gather.2
  93.9 143.3 all-gather.4
  249.3 112.1 all-reduce.2
where the time goes:
time: 371 us
  waiting for transfers between devices  321 us (87%)
  local copies, waits for them, and re-layouts  21.3 us (6%)
  between operations  13.2 us (4%)
  matrix products  8.78 us (2%)
  other arithmetic  5.95 us (2%)
    all_gather x1, waiting for transfers between devices, on_device(): right_full = lax.all_gather(recv_data, 'shot', axis=2, tiled=True)  132 us
    unnamed x4, waiting for transfers between devices  110 us
    all_gather x1, waiting for transfers between devices, on_device(): lax.all_gather(shot_data, 'recv', axis=2, tiled=True)  79.5 us
    unnamed x15, local copies, waits for them, and re-layouts  15.4 us
  transfers between devices with their start and end apart: 3, of which 3 were waited for; matrix products, arithmetic and copies ran while one was open for 5% of the time, Pallas kernels for 0%

commit v1 on v0

--- a/solution.py
+++ b/solution.py
@@ -1,9 +1,20 @@
+import functools
 import jax
 import jax.numpy as jnp
 from jax import lax
 from jax.sharding import PartitionSpec as P
 
 R = 2048
+
+
+def _load_stops_all(view, d0):
+    current_block = jnp.concatenate(
+        jax.lax.all_to_all(jnp.stack(jax.lax.axis_size("shot") * [view]), "shot", 0, 0), axis=d0
+    )
+    return current_block
+
+
+_arrange_rows = functools.partial(_load_stops_all, d0=2)
 
 
 def panel_product(left_operand, right_operand):
@@ -29,7 +40,7 @@
 def on_device(
     shot_data, recv_data, shot_offset, recv_offset, shot_taper_index, receiver_taper_index
 ):
-    right_full = lax.all_gather(recv_data, "shot", axis=2, tiled=True)
+    right_full = _arrange_rows(recv_data)
     partial_sum = make_folder(right_full, lax.all_gather(shot_data, "recv", axis=2, tiled=True))
     multiples = lax.psum_scatter(partial_sum, "surf", scatter_dimension=0, tiled=True)
     shot_row_block = shot_offset.shape[0]

time: 371 us -> 327 us (0.88)
  waiting for transfers between devices: 321 us -> 251 us
  starting transfers between devices: 0.09 us -> 13.4 us
  local copies, waits for them, and re-layouts: 21.3 us -> 28.2 us
  matrix products: 8.78 us -> 14.2 us
    all_gather x1 -> x0, waiting for transfers between devices: 132 us -> none  [on_device(): right_full = lax.all_gather(recv_data, 'shot', axis=2, tiled=True)]
    all_gather x1, waiting for transfers between devices: 79.5 us -> 0.65 us  [on_device(): lax.all_gather(shot_data, 'recv', axis=2, tiled=True)]
    all_to_all x0 -> x1, waiting for transfers between devices: none -> 72.5 us  [_load_stops_all(): jax.lax.all_to_all(jnp.stack(jax.lax.axis_size('shot') * [view]), 'shot',...]
    unnamed x4 -> x3, waiting for transfers between devices: 110 us -> 178 us
    all_to_all x0 -> x1, starting transfers between devices: none -> 13.4 us  [_load_stops_all(): jax.lax.all_to_all(jnp.stack(jax.lax.axis_size('shot') * [view]), 'shot',...]
    reshape x0 -> x1, local copies, waits for them, and re-layouts: none -> 6.06 us  [_load_stops_all(): jnp.concatenate(jax.lax.all_to_all(jnp.stack(jax.lax.axis_size('shot') *...]
    unnamed x15 -> x23, local copies, waits for them, and re-layouts: 15.4 us -> 12.8 us
  transfers between devices with their start and end apart: 3 -> 3, of which waited for: 3 -> 3; matrix products, arithmetic and copies ran while one was open for 5% -> 3% of each run, Pallas kernels for 0% -> 0%
where the time goes in v1:
time: 327 us; the launch traced here: 326 us
  waiting for transfers between devices  251 us (77%)
  local copies, waits for them, and re-layouts  28.2 us (9%)
  matrix products  14.2 us (4%)
  between operations  13.5 us (4%)
  starting transfers between devices  13.4 us (4%)
  other arithmetic  5.89 us (2%)
    unnamed x3, waiting for transfers between devices  178 us
    all_to_all x1, waiting for transfers between devices, _load_stops_all(): jax.lax.all_to_all(jnp.stack(jax.lax.axis_size('shot') * [view]), 'shot',...  72.5 us
    all_to_all x1, starting transfers between devices, _load_stops_all(): jax.lax.all_to_all(jnp.stack(jax.lax.axis_size('shot') * [view]), 'shot',...  13.4 us
    unnamed x23, local copies, waits for them, and re-layouts  12.8 us
  transfers between devices with their start and end apart: 3, of which 3 were waited for; matrix products, arithmetic and copies ran while one was open for 3% of the time, Pallas kernels for 0%

profile of v1, /device:TPU:2, one launch (start us, length us, event | category | flops | bytes accessed | tf_op | source)
XLA Modules:
  0.0 326.2 jit_solution(2209349870556801867)
XLA Ops:
  6.5 1.2 copy.12
  7.7 3.4 %stack.8 = bf16[8,8,2,96,256]{4,3,1,2,0:T(8,128)(2,1)} broadcast(bf16[8,2,96,256]{3,2,0,1:T(8,128)(2,1)S(1)} %copy.12), dimensions={1,2,3,4} | broadcast | bytes 7077888 | tf_op jit(solution)/shard_map/stack | solution.py:12
  11.2 13.4 %all-to-all-start = ((bf16[8,8,2,96,256]{4,3,1,2,0:T(8,128)(2,1)}), bf16[8,8,2,96,256]{4,3,1,2,0:T(8,128)(2,1)}, u32[]{:S(2)}, u32[]{:S(2)}) async-start(bf16[8,8,2,96,256]{4,3,1,2,0:T(8,128)(2,1)} %stack.8), calls=%async_computation | async-start | bytes 12582912 | tf_op jit(solution)/shard_map/all_to_all | solution.py:12
  24.6 0.0 all-gather.2.cloned.1.call-start
  24.6 0.0 copy-done.2
  24.6 1.3 copy.10
  25.9 0.0 all-gather.2.cloned.1.call-update
  25.9 0.0 all-reduce.3.cloned.1.call-start
  26.0 72.5 %all-to-all-done = bf16[8,8,2,96,256]{4,3,1,2,0:T(8,128)(2,1)} async-done(((bf16[8,8,2,96,256]{4,3,1,2,0:T(8,128)(2,1)}), bf16[8,8,2,96,256]{4,3,1,2,0:T(8,128)(2,1)}, u32[]{:S(2)}, u32[]{:S(2)}) %all-to-all-start) | async-done | bytes 6291488 | tf_op jit(solution)/shard_map/all_to_all | solution.py:12
  98.5 6.1 %copy.13 = bf16[8,2,8,96,256]{4,3,2,0,1:T(8,128)(2,1)} copy(bf16[8,2,8,96,256]{4,3,0,1,2:T(8,128)(2,1)} %bitcast.1) | data formatting | bytes 12582912 | tf_op jit(solution)/shard_map/reshape | solution.py:11
  104.5 0.7 all-gather.2.cloned.1.call-done
  105.2 5.8 %fusion.13 = (bf16[8,1,768,256]{3,0,1,2:T(8,128)(2,1)}, bf16[8,1,768,256]{3,0,1,2:T(8,128)(2,1)}) fusion(bf16[8,2,768,256]{3,0,1,2:T(8,128)(2,1)} %all-gather.2.cloned.1.call-done), kind=kLoop, calls=%fused_computation.19 | loop fusion | bytes 12582912 | tf_op jit(solution)/shard_map/slice | solution.py:22
  111.0 5.3 %copy.19 = bf16[8,1,768,256]{2,3,0,1:T(8,128)(2,1)} copy(bf16[8,1,768,256]{3,0,1,2:T(8,128)(2,1)} %get-tuple-element.6) | data formatting | bytes 6291456
  116.3 5.3 %fusion.2 = f32[8,256,256]{2,1,0:T(8,128)} fusion(bf16[8,1,768,256]{2,3,0,1:T(8,128)(2,1)} %copy.19, bf16[8,2,768,256]{3,2,0,1:T(8,128)(2,1)} %bitcast.41), kind=kOutput, calls=%fused_computation.5 | convolution fusion | flops 805306368 | bytes 8388608 | tf_op jit(solution)/shard_map/xaq,xad->xqd/dot_general | solution.py:24
  121.6 0.0 slice-done
  121.6 0.0 slice-done.1
  121.6 0.0 copy-done
  121.6 2.4 fusion
  124.0 3.8 %copy.18 = bf16[8,1,768,256]{2,3,0,1:T(8,128)(2,1)S(1)} copy(bf16[8,1,768,256]{3,0,1,2:T(8,128)(2,1)} %get-tuple-element.5) | data formatting | bytes 6291456
  127.7 0.0 copy-start.1
  127.8 3.7 %subtract_bitcast_fusion = f32[8,1,256,256]{3,2,0,1:T(8,128)S(1)} fusion(f32[8,256,256]{2,1,0:T(8,128)} %fusion.2, bf16[8,2,768,256]{3,2,0,1:T(8,128)(2,1)} %bitcast.42, bf16[8,1,768,256]{2,3,0,1:T(8,128)(2,1)S(1)} %copy.18), kind=kOutput, calls=%fused_computation.12 | convolution fusion | flops 805830656 | bytes 10485760 | tf_op jit(solution)/shard_map/xaq,xad->xqd/dot_general | solution.py:21
  131.4 0.0 copy-done.1
  131.4 2.9 add_bitcast_fusion
  134.3 2.4 pad_maximum_fusion
  136.7 0.0 all-reduce.3.cloned.1.call-update
  136.7 1.3 dynamic-slice
  138.0 0.0 copy-done.6
  138.0 0.0 copy-done.4
  138.0 0.0 copy-done.5
  138.0 1.1 add_multiply_fusion
  139.1 177.8 %all-reduce.3.cloned.1.call-done = f32[8,2,256,256]{3,2,0,1:T(8,128)} async-done(((f32[8,2,256,256]{3,2,0,1:T(8,128)}), f32[8,2,256,256]{3,2,0,1:T(8,128)}) %all-reduce.3.cloned.1.call-update) | async-done | bytes 4194320
  316.9 2.4 fusion.12
  (12 shorter events, 0.0 us)
Async XLA Ops:
  11.2 13.4 %copy-start.2 = (bf16[8,2,96,256]{3,2,1,0:T(8,128)(2,1)S(1)}, bf16[8,2,96,256]{3,2,1,0:T(8,128)(2,1)}, u32[]{:S(2)}) copy-start(bf16[8,2,96,256]{3,2,1,0:T(8,128)(2,1)} %param.6) | copy-start | bytes 2359300
  11.2 87.3 %all-to-all-start = ((bf16[8,8,2,96,256]{4,3,1,2,0:T(8,128)(2,1)}), bf16[8,8,2,96,256]{4,3,1,2,0:T(8,128)(2,1)}, u32[]{:S(2)}, u32[]{:S(2)}) async-start(bf16[8,8,2,96,256]{4,3,1,2,0:T(8,128)(2,1)} %stack.8), calls=%async_computation | async-start | bytes 12582912 | tf_op jit(solution)/shard_map/all_to_all | solution.py:12
  24.6 80.6 %all-gather.2.cloned.1.call-start = ((), (), s32[]{:S(2)}) async-start(), calls=%async_computation.1 | async-start | bytes 7077888 | tf_op jit(solution)/shard_map/all_gather | solution.py:44
  25.9 291.0 %all-reduce.3.cloned.1.call-start = ((), (), s32[]{:S(2)}) async-start(), calls=%async_computation.2 | async-start | bytes 8388608
  111.0 10.6 %slice-start = ((s8[6291456]{0:T(1024)(128)(4,1)}), s8[2097152]{0:T(1024)(128)(4,1)S(1)}, s32[]{:S(2)}) async-start(s8[6291456]{0:T(1024)(128)(4,1)} %bitcast.44), calls=%async_computation.3 | async-start | bytes 4194304
  116.3 5.3 %slice-start.1 = ((s8[6291456]{0:T(1024)(128)(4,1)}), s8[4194304]{0:T(1024)(128)(4,1)S(1)}, s32[]{:S(2)}) async-start(s8[6291456]{0:T(1024)(128)(4,1)} %bitcast.44), calls=%async_computation.4 | async-start | bytes 8388608
  116.3 5.3 %copy-start = (bf16[8,1,768,256]{2,3,0,1:T(8,128)(2,1)S(1)}, bf16[8,1,768,256]{2,3,0,1:T(8,128)(2,1)}, u32[]{:S(2)}) copy-start(bf16[8,1,768,256]{2,3,0,1:T(8,128)(2,1)} %copy.19) | copy-start | bytes 9437188
  127.7 3.7 %copy-start.1 = (f32[8,256,256]{2,1,0:T(8,128)S(1)}, f32[8,256,256]{2,1,0:T(8,128)}, u32[]{:S(2)}) copy-start(f32[8,256,256]{2,1,0:T(8,128)} %fusion) | copy-start | bytes 6291460
  136.7 1.3 copy-start.6
  136.7 1.3 copy-start.4
  136.7 1.3 copy-start.5
  136.7 1.3 copy-start.3
Sparse Core Ops, SparseCore 0:
  27.5 77.6 all-gather.1
  136.8 180.0 all-reduce.2
